TPU v7x, 32 devices: a whole 2x2x4 slice. The times are simulated.
32 devices in a mesh: tm: 8 (over z, x), col: 4 (over y, core).
Axes of the slice: x: 2, y: 2, z: 4, core: 2. Of those that a mesh axis runs over, the one named last changes fastest.
Arguments:
- jacobians: float32 [96, 512, 512], P('tm'), may hold values from -0.05 to 1.05
- increments: float32 [96, 512], P('tm'), may hold values from -1.5 to 1.5
- initial: float32 [512], P('col'), may hold values from -6 to 6
Outputs:
- states: float32 [96, 512], P('tm', 'col')
All inputs are finite; a program needn't handle non-finite values.
Results may differ from a plain program's by a relative error of at most 0.0003.
Values sent between devices are 32-bit elements; how exact they have to be, the bound alone decides.
No kernel may reach another device: no remote copies, remote signals or barrier semaphores. Data moves between devices by JAX's collectives and lax.ppermute only.
A program may use at most 128 MiB of HBM per device.

v0:
```python
import jax
import jax.numpy as jnp
from jax import lax
from jax.sharding import PartitionSpec as P


def from_behind(block, axis, distance):
    devices = range(lax.axis_size(axis))
    route = [(i - distance, i) for i in devices if i - distance in devices]
    return lax.ppermute(block, axis, route)


def matmul(left, right):
    return jnp.dot(left, right, precision=lax.Precision.HIGHEST, preferred_element_type=jnp.float32)


def body(jacobians, increments, initial):
    part_cols = initial.shape[0]
    column_index = lax.axis_index("col")
    segment_index = lax.axis_index("tm")
    rounds = (lax.axis_size("tm") - 1).bit_length()
    first_col = column_index * part_cols

    def own_cols(matrix):
        return lax.dynamic_slice_in_dim(matrix, first_col, part_cols, matrix.ndim - 1)

    def advance_map(running, inputs):
        step_jac, step_inc = inputs
        return ((matmul(step_jac, running[0]), matmul(step_jac, running[1]) + step_inc), None)

    composed, _ = lax.scan(
        advance_map, (own_cols(jacobians[0]), increments[0]), (jacobians[1:], increments[1:])
    )
    acc_map, acc_off = composed
    for level_index in range(rounds):
        distance = 1 << level_index
        recv_map, recv_off = from_behind((acc_map, acc_off), "tm", distance)

        def fold_columns(running, col_block, first_row, recv_map=recv_map, recv_off=recv_off):
            return (matmul(col_block, recv_map), running[1] + matmul(col_block, recv_off))

        new_map, new_off = fold_columns(
            (jnp.zeros_like(acc_map), acc_off),
            lax.all_gather(acc_map, "col", axis=1, tiled=True),
            jnp.int32(0),
        )
        active = segment_index >= distance
        acc_map = jnp.where(active, new_map, acc_map)
        acc_off = jnp.where(active, new_off, acc_off)
    end_part = matmul(acc_map, initial)
    end_mine = lax.psum_scatter(end_part, "col", scatter_dimension=0, tiled=True) + own_cols(
        acc_off
    )
    handed = from_behind(end_mine, "tm", 1)
    start_mine = jnp.where(segment_index == 0, initial, handed)
    start_full = lax.all_gather(start_mine, "col", axis=0, tiled=True)

    def advance_state(current, inputs):
        step_jac, step_inc = inputs
        following = matmul(step_jac, current) + step_inc
        return (following, own_cols(following))

    _, leading = lax.scan(advance_state, start_full, (jacobians[:-1], increments[:-1]))
    return jnp.concatenate([leading, end_mine[None, :]], axis=0)


def solution(mesh):
    return jax.shard_map(
        body,
        mesh=mesh,
        in_specs=(P("tm", None, None), P("tm", None), P("col")),
        out_specs=P("tm", "col"),
        check_vma=False,
    )
```

profile of v0, /device:TPU:25, one launch (start us, length us, event | category | flops | bytes accessed | tf_op | source)
XLA Modules:
  0.0 202.7 jit_solution(5260583161376502509)
XLA Ops:
  6.5 17.6 %fusion.15 = (f32[11,512,512]{2,1,0:T(8,128)}, f32[11,512,512]{2,1,0:T(8,128)}) fusion(f32[12,512,512]{2,1,0:T(8,128)} %param.7), kind=kLoop, calls=%fused_computation.28 | loop fusion | bytes 46137344 | tf_op jit(solution)/shard_map/slice | solution.py:63
  24.2 49.5 %while.26 = (s32[]{:T(128)}, f32[512,128]{1,0:T(8,128)S(1)}, f32[512]{0:T(512)S(1)}, f32[11,512,512]{2,1,0:T(8,128)}, f32[11,512]{1,0:T(8,128)S(1)}, /*index=5*/s32[]{:T(128)}) while((s32[]{:T(128)}, f32[512,128]{1,0:T(8,128)S(1)}, f32[512]{0:T(512)S(1)}, f32[11,512,512]{2,1,0:T(8,128)}, f32[11,512]{1,0:T(8,128)S(1)}, ...), condition=%wide.region_1.2_spmd, body=%wide.region_0.1_spmd.sunk | while | flops 405799424 | bytes 3161161 | solution.py:31
  24.2 2.2 %fusion.50 = f32[1,512]{1,0:T(1,128)S(1)} fusion(f32[512,1]{0,1:T(1,128)S(1)} %bitcast.80, f32[11,512,512]{2,1,0:T(8,128)} %get-tuple-element.219, s32[]{:T(128)} %get-tuple-element.210), kind=kOutput, calls=%fused_computation.clone.1 | convolution fusion | flops 3145728 | bytes 1053184 | tf_op jit(solution)/shard_map/while/body/eval_jaxpr/dot_general | solution.py:14
  26.5 2.2 %fusion.49 = f32[512,128]{1,0:T(8,128)S(1)} fusion(f32[512,128]{1,0:T(8,128)S(1)} %copy.24, f32[11,512,512]{2,1,0:T(8,128)} %get-tuple-element.219, s32[]{:T(128)} %get-tuple-element.210), kind=kOutput, calls=%fused_computation.2.clone.1 | convolution fusion | flops 402653184 | bytes 1573376 | tf_op jit(solution)/shard_map/while/body/eval_jaxpr/dot_general | solution.py:14
  28.7 2.2 %fusion.50 = f32[1,512]{1,0:T(1,128)S(1)} fusion(f32[512,1]{0,1:T(1,128)S(1)} %bitcast.80, f32[11,512,512]{2,1,0:T(8,128)} %get-tuple-element.219, s32[]{:T(128)} %get-tuple-element.210), kind=kOutput, calls=%fused_computation.clone.1 | convolution fusion | flops 3145728 | bytes 1053184 | tf_op jit(solution)/shard_map/while/body/eval_jaxpr/dot_general | solution.py:14
  31.0 2.2 %fusion.49 = f32[512,128]{1,0:T(8,128)S(1)} fusion(f32[512,128]{1,0:T(8,128)S(1)} %copy.24, f32[11,512,512]{2,1,0:T(8,128)} %get-tuple-element.219, s32[]{:T(128)} %get-tuple-element.210), kind=kOutput, calls=%fused_computation.2.clone.1 | convolution fusion | flops 402653184 | bytes 1573376 | tf_op jit(solution)/shard_map/while/body/eval_jaxpr/dot_general | solution.py:14
  33.2 2.2 %fusion.50 = f32[1,512]{1,0:T(1,128)S(1)} fusion(f32[512,1]{0,1:T(1,128)S(1)} %bitcast.80, f32[11,512,512]{2,1,0:T(8,128)} %get-tuple-element.219, s32[]{:T(128)} %get-tuple-element.210), kind=kOutput, calls=%fused_computation.clone.1 | convolution fusion | flops 3145728 | bytes 1053184 | tf_op jit(solution)/shard_map/while/body/eval_jaxpr/dot_general | solution.py:14
  35.5 2.2 %fusion.49 = f32[512,128]{1,0:T(8,128)S(1)} fusion(f32[512,128]{1,0:T(8,128)S(1)} %copy.24, f32[11,512,512]{2,1,0:T(8,128)} %get-tuple-element.219, s32[]{:T(128)} %get-tuple-element.210), kind=kOutput, calls=%fused_computation.2.clone.1 | convolution fusion | flops 402653184 | bytes 1573376 | tf_op jit(solution)/shard_map/while/body/eval_jaxpr/dot_general | solution.py:14
  40.0 2.2 %fusion.49 = f32[512,128]{1,0:T(8,128)S(1)} fusion(f32[512,128]{1,0:T(8,128)S(1)} %copy.24, f32[11,512,512]{2,1,0:T(8,128)} %get-tuple-element.219, s32[]{:T(128)} %get-tuple-element.210), kind=kOutput, calls=%fused_computation.2.clone.1 | convolution fusion | flops 402653184 | bytes 1573376 | tf_op jit(solution)/shard_map/while/body/eval_jaxpr/dot_general | solution.py:14
  42.2 2.2 %fusion.50 = f32[1,512]{1,0:T(1,128)S(1)} fusion(f32[512,1]{0,1:T(1,128)S(1)} %bitcast.80, f32[11,512,512]{2,1,0:T(8,128)} %get-tuple-element.219, s32[]{:T(128)} %get-tuple-element.210), kind=kOutput, calls=%fused_computation.clone.1 | convolution fusion | flops 3145728 | bytes 1053184 | tf_op jit(solution)/shard_map/while/body/eval_jaxpr/dot_general | solution.py:14
  44.5 2.2 %fusion.49 = f32[512,128]{1,0:T(8,128)S(1)} fusion(f32[512,128]{1,0:T(8,128)S(1)} %copy.24, f32[11,512,512]{2,1,0:T(8,128)} %get-tuple-element.219, s32[]{:T(128)} %get-tuple-element.210), kind=kOutput, calls=%fused_computation.2.clone.1 | convolution fusion | flops 402653184 | bytes 1573376 | tf_op jit(solution)/shard_map/while/body/eval_jaxpr/dot_general | solution.py:14
  46.7 2.2 %fusion.50 = f32[1,512]{1,0:T(1,128)S(1)} fusion(f32[512,1]{0,1:T(1,128)S(1)} %bitcast.80, f32[11,512,512]{2,1,0:T(8,128)} %get-tuple-element.219, s32[]{:T(128)} %get-tuple-element.210), kind=kOutput, calls=%fused_computation.clone.1 | convolution fusion | flops 3145728 | bytes 1053184 | tf_op jit(solution)/shard_map/while/body/eval_jaxpr/dot_general | solution.py:14
  49.0 2.2 %fusion.49 = f32[512,128]{1,0:T(8,128)S(1)} fusion(f32[512,128]{1,0:T(8,128)S(1)} %copy.24, f32[11,512,512]{2,1,0:T(8,128)} %get-tuple-element.219, s32[]{:T(128)} %get-tuple-element.210), kind=kOutput, calls=%fused_computation.2.clone.1 | convolution fusion | flops 402653184 | bytes 1573376 | tf_op jit(solution)/shard_map/while/body/eval_jaxpr/dot_general | solution.py:14
  53.5 2.2 %fusion.49 = f32[512,128]{1,0:T(8,128)S(1)} fusion(f32[512,128]{1,0:T(8,128)S(1)} %copy.24, f32[11,512,512]{2,1,0:T(8,128)} %get-tuple-element.219, s32[]{:T(128)} %get-tuple-element.210), kind=kOutput, calls=%fused_computation.2.clone.1 | convolution fusion | flops 402653184 | bytes 1573376 | tf_op jit(solution)/shard_map/while/body/eval_jaxpr/dot_general | solution.py:14
  55.7 2.2 %fusion.50 = f32[1,512]{1,0:T(1,128)S(1)} fusion(f32[512,1]{0,1:T(1,128)S(1)} %bitcast.80, f32[11,512,512]{2,1,0:T(8,128)} %get-tuple-element.219, s32[]{:T(128)} %get-tuple-element.210), kind=kOutput, calls=%fused_computation.clone.1 | convolution fusion | flops 3145728 | bytes 1053184 | tf_op jit(solution)/shard_map/while/body/eval_jaxpr/dot_general | solution.py:14
  58.0 2.2 %fusion.49 = f32[512,128]{1,0:T(8,128)S(1)} fusion(f32[512,128]{1,0:T(8,128)S(1)} %copy.24, f32[11,512,512]{2,1,0:T(8,128)} %get-tuple-element.219, s32[]{:T(128)} %get-tuple-element.210), kind=kOutput, calls=%fused_computation.2.clone.1 | convolution fusion | flops 402653184 | bytes 1573376 | tf_op jit(solution)/shard_map/while/body/eval_jaxpr/dot_general | solution.py:14
  60.2 2.2 %fusion.50 = f32[1,512]{1,0:T(1,128)S(1)} fusion(f32[512,1]{0,1:T(1,128)S(1)} %bitcast.80, f32[11,512,512]{2,1,0:T(8,128)} %get-tuple-element.219, s32[]{:T(128)} %get-tuple-element.210), kind=kOutput, calls=%fused_computation.clone.1 | convolution fusion | flops 3145728 | bytes 1053184 | tf_op jit(solution)/shard_map/while/body/eval_jaxpr/dot_general | solution.py:14
  62.5 2.2 %fusion.49 = f32[512,128]{1,0:T(8,128)S(1)} fusion(f32[512,128]{1,0:T(8,128)S(1)} %copy.24, f32[11,512,512]{2,1,0:T(8,128)} %get-tuple-element.219, s32[]{:T(128)} %get-tuple-element.210), kind=kOutput, calls=%fused_computation.2.clone.1 | convolution fusion | flops 402653184 | bytes 1573376 | tf_op jit(solution)/shard_map/while/body/eval_jaxpr/dot_general | solution.py:14
  67.0 2.2 %fusion.49 = f32[512,128]{1,0:T(8,128)S(1)} fusion(f32[512,128]{1,0:T(8,128)S(1)} %copy.24, f32[11,512,512]{2,1,0:T(8,128)} %get-tuple-element.219, s32[]{:T(128)} %get-tuple-element.210), kind=kOutput, calls=%fused_computation.2.clone.1 | convolution fusion | flops 402653184 | bytes 1573376 | tf_op jit(solution)/shard_map/while/body/eval_jaxpr/dot_general | solution.py:14
  69.2 2.2 %fusion.50 = f32[1,512]{1,0:T(1,128)S(1)} fusion(f32[512,1]{0,1:T(1,128)S(1)} %bitcast.80, f32[11,512,512]{2,1,0:T(8,128)} %get-tuple-element.219, s32[]{:T(128)} %get-tuple-element.210), kind=kOutput, calls=%fused_computation.clone.1 | convolution fusion | flops 3145728 | bytes 1053184 | tf_op jit(solution)/shard_map/while/body/eval_jaxpr/dot_general | solution.py:14
  71.5 2.2 %fusion.49 = f32[512,128]{1,0:T(8,128)S(1)} fusion(f32[512,128]{1,0:T(8,128)S(1)} %copy.24, f32[11,512,512]{2,1,0:T(8,128)} %get-tuple-element.219, s32[]{:T(128)} %get-tuple-element.210), kind=kOutput, calls=%fused_computation.2.clone.1 | convolution fusion | flops 402653184 | bytes 1573376 | tf_op jit(solution)/shard_map/while/body/eval_jaxpr/dot_general | solution.py:14
  74.5 3.1 %collective-permute-start = (f32[512,128]{1,0:T(8,128)}, f32[512,128]{1,0:T(8,128)S(1)}, u32[]{:S(2)}, u32[]{:S(2)}) collective-permute-start(f32[512,128]{1,0:T(8,128)} %copy-done), channel_id=1, source_target_pairs={{0,4},{4,8},{8,12},{12,16},{16,20},{20,24},{24,28},{1,5},{5,9},{9,... | collective-permute-start | bytes 786440 | tf_op jit(solution)/shard_map/ppermute | solution.py:10
  77.7 7.1 %collective-permute-done = f32[512,128]{1,0:T(8,128)S(1)} collective-permute-done((f32[512,128]{1,0:T(8,128)}, f32[512,128]{1,0:T(8,128)S(1)}, u32[]{:S(2)}, u32[]{:S(2)}) %collective-permute-start) | collective-permute-done | bytes 262176 | tf_op jit(solution)/shard_map/ppermute | solution.py:10
  84.7 8.1 %all-gather.5.cloned.1.call-done = f32[512,512]{1,0:T(8,128)} async-done(((f32[512,128]{1,0:T(8,128)}), f32[512,512]{1,0:T(8,128)}) %all-gather.5.cloned.1.call-update) | async-done | bytes 1048592 | tf_op jit(solution)/shard_map/all_gather | solution.py:44
  92.8 2.9 %convolution_select_fusion.2 = f32[512,128]{1,0:T(8,128)} fusion(f32[512,128]{1,0:T(8,128)} %copy-done, f32[512,512]{1,0:T(8,128)} %all-gather.5.cloned.1.call-done, f32[512,128]{1,0:T(8,128)S(1)} %collective-permute-done, pred[]{:T(512)S(6)} %ge.11), kind=kOutput, calls=%fused_computation.17 | convolution fusion | flops 402718720 | bytes 1835009 | tf_op jit(solution)/shard_map/dot_general | solution.py:14
  97.1 8.4 %collective-permute-done.1 = f32[512,128]{1,0:T(8,128)S(1)} collective-permute-done((f32[512,128]{1,0:T(8,128)}, f32[512,128]{1,0:T(8,128)S(1)}, u32[]{:S(2)}, u32[]{:S(2)}) %collective-permute-start.1) | collective-permute-done | bytes 262176 | tf_op jit(solution)/shard_map/ppermute | solution.py:10
  105.5 7.2 %all-gather.7.cloned.1.call-done = f32[512,512]{1,0:T(8,128)} async-done(((f32[512,128]{1,0:T(8,128)}), f32[512,512]{1,0:T(8,128)}) %all-gather.7.cloned.1.call-update) | async-done | bytes 1048592 | tf_op jit(solution)/shard_map/all_gather | solution.py:44
  112.7 2.9 %convolution_select_fusion.1 = f32[512,128]{1,0:T(8,128)} fusion(f32[512,128]{1,0:T(8,128)} %convolution_select_fusion.2, f32[512,512]{1,0:T(8,128)} %all-gather.7.cloned.1.call-done, f32[512,128]{1,0:T(8,128)S(1)} %collective-permute-done.1, pred[]{:T(512)S(6)} %ge.10), kind=kOutput, calls=%fused_computation.16 | convolution fusion | flops 402718720 | bytes 1835009 | tf_op jit(solution)/shard_map/dot_general | solution.py:14
  115.7 3.1 %collective-permute-start.3 = (f32[512]{0:T(512)S(1)}, f32[512]{0:T(512)S(1)}, u32[]{:S(2)}, u32[]{:S(2)}) collective-permute-start(f32[512]{0:T(512)S(1)} %get-tuple-element.108), channel_id=1, source_target_pairs={{0,4},{4,8},{8,12},{12,16},{16,20},{20,24},{24,28},{1,5},{5,9},{9,... | collective-permute-start | bytes 6152 | tf_op jit(solution)/shard_map/ppermute | solution.py:10
  120.9 2.2 %fusion.17 = f32[1,512]{1,0:T(1,128)S(1)} fusion(f32[512,512]{1,0:T(8,128)} %all-gather.5.cloned.1.call-done, f32[512,1]{0,1:T(1,128)S(1)} %bitcast.89), kind=kOutput, calls=%fused_computation.30 | convolution fusion | flops 3145728 | bytes 1052672 | tf_op jit(solution)/shard_map/dot_general | solution.py:14
  124.5 3.4 %collective-permute-done.4 = f32[512]{0:T(512)S(1)} collective-permute-done((f32[512]{0:T(512)S(1)}, f32[512]{0:T(512)S(1)}, u32[]{:S(2)}, u32[]{:S(2)}) %collective-permute-start.4) | collective-permute-done | bytes 2080 | tf_op jit(solution)/shard_map/ppermute | solution.py:10
  127.9 2.3 %fusion.18 = f32[1,512]{1,0:T(1,128)S(1)} fusion(f32[512,512]{1,0:T(8,128)} %all-gather.7.cloned.1.call-done, f32[512,1]{0,1:T(1,128)S(1)} %bitcast.90), kind=kOutput, calls=%fused_computation.31 | convolution fusion | flops 3145728 | bytes 1052672 | tf_op jit(solution)/shard_map/dot_general | solution.py:14
  137.6 11.9 %collective-permute-done.2 = f32[512,128]{1,0:T(8,128)S(1)} collective-permute-done((f32[512,128]{1,0:T(8,128)}, f32[512,128]{1,0:T(8,128)S(1)}, u32[]{:S(2)}, u32[]{:S(2)}) %collective-permute-start.2) | collective-permute-done | bytes 262176 | tf_op jit(solution)/shard_map/ppermute | solution.py:10
  149.5 2.2 %convolution_select_fusion = f32[512,128]{1,0:T(8,128)S(1)} fusion(f32[512,128]{1,0:T(8,128)} %convolution_select_fusion.1, f32[512,512]{1,0:T(8,128)} %all-gather.9.cloned.1.call-done, f32[512,128]{1,0:T(8,128)S(1)} %collective-permute-done.2, pred[]{:T(512)S(6)} %ge.9), kind=kOutput, calls=%fused_computation.15 | convolution fusion | flops 402718720 | bytes 1835009 | tf_op jit(solution)/shard_map/dot_general | solution.py:14
  152.1 5.5 %all-reduce = f32[512]{0:T(512)S(1)} all-reduce(f32[512]{0:T(512)S(1)} %bitcast.87), channel_id=2, replica_groups=mesh['tm'=8,'col'=4] {'col'}, use_global_device_ids=true, to_apply=%region_2.3.clone | all-reduce | flops 512 | bytes 4096
  159.8 3.1 %collective-permute-done.6 = f32[128]{0:T(128)S(1)} collective-permute-done((f32[128]{0:T(128)S(1)}, f32[128]{0:T(128)S(1)}, u32[]{:S(2)}, u32[]{:S(2)}) %collective-permute-start.6) | collective-permute-done | bytes 544 | tf_op jit(solution)/shard_map/ppermute | solution.py:10
  162.9 6.9 %all-gather = f32[4,1,128]{2,1,0:T(1,128)S(1)} all-gather(f32[1,1,128]{2,1,0:T(1,128)S(1)} %fusion.12), channel_id=1, replica_groups=mesh['tm'=8,'col'=4] {'col'}, dimensions={0}, use_global_device_ids=true | all-gather | bytes 2560 | tf_op jit(solution)/shard_map/all_gather | solution.py:56
  169.8 25.8 %while.27 = (s32[]{:T(128)}, f32[512]{0:T(512)S(1)}, f32[11,128]{1,0:T(8,128)S(1)}, f32[11,512,512]{2,1,0:T(8,128)}, f32[11,512]{1,0:T(8,128)S(1)}, /*index=5*/s32[]{:T(128)}, s32[]{:T(128)}, s32[]{:T(128)}) while((s32[]{:T(128)}, f32[512]{0:T(512)S(1)}, f32[11,128]{1,0:T(8,128)S(1)}, f32[11,512,512]{2,1,0:T(8,128)}, f32[11,512]{1,0:T(8,128)S(1)}, ...), condition=%wide.region_4.5_spmd, body=%wide.region_3.4_spmd.sunk | while | flops 3146242 | bytes 1065569 | solution.py:63
  172.1 2.2 %fusion.53 = f32[1,512]{1,0:T(1,128)S(1)} fusion(f32[512,1]{0,1:T(1,128)S(1)} %bitcast.83, f32[11,512,512]{2,1,0:T(8,128)} %get-tuple-element.241, s32[]{:T(128)} %get-tuple-element.230), kind=kOutput, calls=%fused_computation.9.clone.1 | convolution fusion | flops 3145728 | bytes 1053184 | tf_op jit(solution)/shard_map/while/body/eval_jaxpr/dot_general | solution.py:14
  174.5 2.2 %fusion.53 = f32[1,512]{1,0:T(1,128)S(1)} fusion(f32[512,1]{0,1:T(1,128)S(1)} %bitcast.83, f32[11,512,512]{2,1,0:T(8,128)} %get-tuple-element.241, s32[]{:T(128)} %get-tuple-element.230), kind=kOutput, calls=%fused_computation.9.clone.1 | convolution fusion | flops 3145728 | bytes 1053184 | tf_op jit(solution)/shard_map/while/body/eval_jaxpr/dot_general | solution.py:14
  176.8 2.2 %fusion.53 = f32[1,512]{1,0:T(1,128)S(1)} fusion(f32[512,1]{0,1:T(1,128)S(1)} %bitcast.83, f32[11,512,512]{2,1,0:T(8,128)} %get-tuple-element.241, s32[]{:T(128)} %get-tuple-element.230), kind=kOutput, calls=%fused_computation.9.clone.1 | convolution fusion | flops 3145728 | bytes 1053184 | tf_op jit(solution)/shard_map/while/body/eval_jaxpr/dot_general | solution.py:14
  179.2 2.2 %fusion.53 = f32[1,512]{1,0:T(1,128)S(1)} fusion(f32[512,1]{0,1:T(1,128)S(1)} %bitcast.83, f32[11,512,512]{2,1,0:T(8,128)} %get-tuple-element.241, s32[]{:T(128)} %get-tuple-element.230), kind=kOutput, calls=%fused_computation.9.clone.1 | convolution fusion | flops 3145728 | bytes 1053184 | tf_op jit(solution)/shard_map/while/body/eval_jaxpr/dot_general | solution.py:14
  181.5 2.2 %fusion.53 = f32[1,512]{1,0:T(1,128)S(1)} fusion(f32[512,1]{0,1:T(1,128)S(1)} %bitcast.83, f32[11,512,512]{2,1,0:T(8,128)} %get-tuple-element.241, s32[]{:T(128)} %get-tuple-element.230), kind=kOutput, calls=%fused_computation.9.clone.1 | convolution fusion | flops 3145728 | bytes 1053184 | tf_op jit(solution)/shard_map/while/body/eval_jaxpr/dot_general | solution.py:14
  183.9 2.2 %fusion.53 = f32[1,512]{1,0:T(1,128)S(1)} fusion(f32[512,1]{0,1:T(1,128)S(1)} %bitcast.83, f32[11,512,512]{2,1,0:T(8,128)} %get-tuple-element.241, s32[]{:T(128)} %get-tuple-element.230), kind=kOutput, calls=%fused_computation.9.clone.1 | convolution fusion | flops 3145728 | bytes 1053184 | tf_op jit(solution)/shard_map/while/body/eval_jaxpr/dot_general | solution.py:14
  186.2 2.2 %fusion.53 = f32[1,512]{1,0:T(1,128)S(1)} fusion(f32[512,1]{0,1:T(1,128)S(1)} %bitcast.83, f32[11,512,512]{2,1,0:T(8,128)} %get-tuple-element.241, s32[]{:T(128)} %get-tuple-element.230), kind=kOutput, calls=%fused_computation.9.clone.1 | convolution fusion | flops 3145728 | bytes 1053184 | tf_op jit(solution)/shard_map/while/body/eval_jaxpr/dot_general | solution.py:14
  188.6 2.2 %fusion.53 = f32[1,512]{1,0:T(1,128)S(1)} fusion(f32[512,1]{0,1:T(1,128)S(1)} %bitcast.83, f32[11,512,512]{2,1,0:T(8,128)} %get-tuple-element.241, s32[]{:T(128)} %get-tuple-element.230), kind=kOutput, calls=%fused_computation.9.clone.1 | convolution fusion | flops 3145728 | bytes 1053184 | tf_op jit(solution)/shard_map/while/body/eval_jaxpr/dot_general | solution.py:14
  190.9 2.2 %fusion.53 = f32[1,512]{1,0:T(1,128)S(1)} fusion(f32[512,1]{0,1:T(1,128)S(1)} %bitcast.83, f32[11,512,512]{2,1,0:T(8,128)} %get-tuple-element.241, s32[]{:T(128)} %get-tuple-element.230), kind=kOutput, calls=%fused_computation.9.clone.1 | convolution fusion | flops 3145728 | bytes 1053184 | tf_op jit(solution)/shard_map/while/body/eval_jaxpr/dot_general | solution.py:14
  193.3 2.2 %fusion.53 = f32[1,512]{1,0:T(1,128)S(1)} fusion(f32[512,1]{0,1:T(1,128)S(1)} %bitcast.83, f32[11,512,512]{2,1,0:T(8,128)} %get-tuple-element.241, s32[]{:T(128)} %get-tuple-element.230), kind=kOutput, calls=%fused_computation.9.clone.1 | convolution fusion | flops 3145728 | bytes 1053184 | tf_op jit(solution)/shard_map/while/body/eval_jaxpr/dot_general | solution.py:14
  (119 shorter events, 26.2 us)
Async XLA Ops:
  6.5 86.3 %all-gather.5.cloned.1.call-start = ((), (), s32[]{:S(2)}) async-start(), calls=%async_computation | async-start | bytes 1310720 | tf_op jit(solution)/shard_map/all_gather | solution.py:44
  6.5 17.6 %copy-start.1 = (f32[12,512]{1,0:T(8,128)S(1)}, f32[12,512]{1,0:T(8,128)}, u32[]{:S(2)}) copy-start(f32[12,512]{1,0:T(8,128)} %param.8) | copy-start | bytes 73732
  6.5 17.6 %slice-start = ((f32[12,512,512]{2,1,0:T(8,128)}), f32[1,512,512]{2,1,0:T(8,128)S(1)}, s32[]{:S(2)}) async-start(f32[12,512,512]{2,1,0:T(8,128)} %param.7), calls=%async_computation.3 | async-start | bytes 2097152 | tf_op jit(solution)/shard_map/slice | solution.py:32
  6.5 17.7 %slice-start.1 = ((f32[12,512]{1,0:T(8,128)}), f32[1,512]{1,0:T(1,128)S(1)}, s32[]{:S(2)}) async-start(f32[12,512]{1,0:T(8,128)} %param.8), calls=%async_computation.4 | async-start | bytes 4096 | tf_op jit(solution)/shard_map/slice | solution.py:32
  24.1 107.3 %copy-start.3 = (u32[32]{0:T(128)S(1)}, u32[32]{0:T(128)}, u32[]{:S(2)}) copy-start(u32[32]{0:T(128)} %constant.58) | copy-start | bytes 388
  24.2 127.5 %copy-start.2 = (f32[128]{0:T(128)S(1)}, f32[128]{0:T(128)}, u32[]{:S(2)}) copy-start(f32[128]{0:T(128)} %param.9) | copy-start | bytes 1540
  73.7 0.7 copy-start
  74.5 38.3 %all-gather.7.cloned.1.call-start = ((), (), s32[]{:S(2)}) async-start(), calls=%async_computation.1 | async-start | bytes 1310720 | tf_op jit(solution)/shard_map/all_gather | solution.py:44
  74.5 10.2 %collective-permute-start = (f32[512,128]{1,0:T(8,128)}, f32[512,128]{1,0:T(8,128)S(1)}, u32[]{:S(2)}, u32[]{:S(2)}) collective-permute-start(f32[512,128]{1,0:T(8,128)} %copy-done), channel_id=1, source_target_pairs={{0,4},{4,8},{8,12},{12,16},{16,20},{20,24},{24,28},{1,5},{5,9},{9,... | collective-permute-start | bytes 786440 | tf_op jit(solution)/shard_map/ppermute | solution.py:10
  95.8 39.6 %all-gather.9.cloned.1.call-start = ((), (), s32[]{:S(2)}) async-start(), calls=%async_computation.2 | async-start | bytes 1310720 | tf_op jit(solution)/shard_map/all_gather | solution.py:44
  95.8 9.7 %collective-permute-start.1 = (f32[512,128]{1,0:T(8,128)}, f32[512,128]{1,0:T(8,128)S(1)}, u32[]{:S(2)}, u32[]{:S(2)}) collective-permute-start(f32[512,128]{1,0:T(8,128)} %convolution_select_fusion.2), channel_id=1, source_target_pairs={{0,8},{4,12},{8,16},{12,20},{16,24},{20,28},{1,9},{5,13},{9,17},{1... | collective-permute-start | bytes 786440 | tf_op jit(solution)/shard_map/ppermute | solution.py:10
  115.7 5.2 %collective-permute-start.3 = (f32[512]{0:T(512)S(1)}, f32[512]{0:T(512)S(1)}, u32[]{:S(2)}, u32[]{:S(2)}) collective-permute-start(f32[512]{0:T(512)S(1)} %get-tuple-element.108), channel_id=1, source_target_pairs={{0,4},{4,8},{8,12},{12,16},{16,20},{20,24},{24,28},{1,5},{5,9},{9,... | collective-permute-start | bytes 6152 | tf_op jit(solution)/shard_map/ppermute | solution.py:10
  123.2 4.7 %collective-permute-start.4 = (f32[512]{0:T(512)S(1)}, f32[512]{0:T(512)S(1)}, u32[]{:S(2)}, u32[]{:S(2)}) collective-permute-start(f32[512]{0:T(512)S(1)} %add_select_fusion.2), channel_id=1, source_target_pairs={{0,8},{4,12},{8,16},{12,20},{16,24},{20,28},{1,9},{5,13},{9,17},{1... | collective-permute-start | bytes 6152 | tf_op jit(solution)/shard_map/ppermute | solution.py:10
  130.2 5.2 %collective-permute-start.5 = (f32[512]{0:T(512)S(1)}, f32[512]{0:T(512)S(1)}, u32[]{:S(2)}, u32[]{:S(2)}) collective-permute-start(f32[512]{0:T(512)S(1)} %add_select_fusion.1), channel_id=1, source_target_pairs={{0,16},{4,20},{8,24},{12,28},{1,17},{5,21},{9,25},{13,29},{2,18},{... | collective-permute-start | bytes 6152 | tf_op jit(solution)/shard_map/ppermute | solution.py:10
  132.7 16.8 %collective-permute-start.2 = (f32[512,128]{1,0:T(8,128)}, f32[512,128]{1,0:T(8,128)S(1)}, u32[]{:S(2)}, u32[]{:S(2)}) collective-permute-start(f32[512,128]{1,0:T(8,128)} %convolution_select_fusion.1), channel_id=1, source_target_pairs={{0,16},{4,20},{8,24},{12,28},{1,17},{5,21},{9,25},{13,29},{2,18},{... | collective-permute-start | bytes 786440 | tf_op jit(solution)/shard_map/ppermute | solution.py:10
  157.7 5.2 %collective-permute-start.6 = (f32[128]{0:T(128)S(1)}, f32[128]{0:T(128)S(1)}, u32[]{:S(2)}, u32[]{:S(2)}) collective-permute-start(f32[128]{0:T(128)S(1)} %dynamic-slice_add_fusion), channel_id=1, source_target_pairs={{0,4},{4,8},{8,12},{12,16},{16,20},{20,24},{24,28},{1,5},{5,9},{9,... | collective-permute-start | bytes 1544 | tf_op jit(solution)/shard_map/ppermute | solution.py:10
Sparse Core Ops, SparseCore 0:
  74.6 18.1 all-gather.4
  95.9 16.8 all-gather.6
  115.8 16.8 all-gather.8
where the time goes:
time: 205 us; the launch traced here: 203 us
  matrix products  87.8 us (43%)
  waiting for transfers between devices  52.8 us (26%)
  local copies, waits for them, and re-layouts  20.7 us (10%)
  between operations  14 us (7%)
  starting transfers between devices  13.6 us (7%)
  blocking collectives  12.4 us (6%)
    dot_general x40, matrix products, matmul(): jnp.dot(left, right, precision=lax.Precision.HIGHEST, preferred_element_t...  87.8 us
    ppermute x7, waiting for transfers between devices, from_behind(): return lax.ppermute(block, axis, route)  37.4 us
    slice x1, local copies, waits for them, and re-layouts, body(): jacobians[:-1]  17.6 us
    all_gather x3, waiting for transfers between devices, body(): lax.all_gather(acc_map, 'col', axis=1, tiled=True)  15.3 us
    ppermute x7, starting transfers between devices, from_behind(): return lax.ppermute(block, axis, route)  13.5 us
    all_gather x1, blocking collectives, body(): start_full = lax.all_gather(start_mine, 'col', axis=0, tiled=True)  6.9 us
    unnamed x1, blocking collectives  5.5 us
  transfers between devices with their start and end apart: 10, of which 9 were waited for; matrix products, arithmetic and copies ran while one was open for 4% of the time, Pallas kernels for 0%

commit v1 on v0

--- a/solution.py
+++ b/solution.py
@@ -2,6 +2,14 @@
 import jax.numpy as jnp
 from jax import lax
 from jax.sharding import PartitionSpec as P
+
+
+def tiled_gather(shard, axis, dim):
+    size = lax.axis_size(axis)
+    repeats = [size if d == dim else 1 for d in range(shard.ndim)]
+    return lax.all_to_all(
+        jnp.tile(shard, repeats), axis, split_axis=dim, concat_axis=dim, tiled=True
+    )
 
 
 def from_behind(block, axis, distance):
@@ -40,9 +48,7 @@
             return (matmul(col_block, recv_map), running[1] + matmul(col_block, recv_off))
 
         new_map, new_off = fold_columns(
-            (jnp.zeros_like(acc_map), acc_off),
-            lax.all_gather(acc_map, "col", axis=1, tiled=True),
-            jnp.int32(0),
+            (jnp.zeros_like(acc_map), acc_off), tiled_gather(acc_map, "col", 1), jnp.int32(0)
         )
         active = segment_index >= distance
         acc_map = jnp.where(active, new_map, acc_map)

time: 205 us -> 190 us (0.927)
  starting transfers between devices: 13.6 us -> 27.7 us
  waiting for transfers between devices: 52.8 us -> 39 us
  between operations: 14 us -> 0.91 us
  matrix products: 87.8 us -> 81.4 us
  local copies, waits for them, and re-layouts: 20.7 us -> 24.2 us
    all_to_all x0 -> x3, waiting for transfers between devices: none -> 23.1 us  [tiled_gather(): lax.all_to_all(jnp.tile(shard, repeats), axis, split_axis=dim, concat_axi...]
    ppermute x7, waiting for transfers between devices: 37.4 us -> 15.9 us  [from_behind(): return lax.ppermute(block, axis, route)]
    all_gather x3 -> x0, waiting for transfers between devices: 15.3 us -> none  [body(): lax.all_gather(acc_map, 'col', axis=1, tiled=True)]
    all_to_all x0 -> x3, starting transfers between devices: none -> 13.2 us  [tiled_gather(): lax.all_to_all(jnp.tile(shard, repeats), axis, split_axis=dim, concat_axi...]
    dot_general x40, matrix products: 87.8 us -> 81.4 us  [matmul(): jnp.dot(left, right, precision=lax.Precision.HIGHEST, preferred_element_t...]
    another operation x0 -> x3, local copies, waits for them, and re-layouts: none -> 3.22 us  [tiled_gather(): jnp.tile(shard, repeats)]
  transfers between devices with their start and end apart: 10 -> 10, of which waited for: 9 -> 6; matrix products, arithmetic and copies ran while one was open for 4% -> 4% of each run, Pallas kernels for 0% -> 0%
where the time goes in v1:
time: 190 us; the launch traced here: 188 us
  matrix products  81.4 us (43%)
  waiting for transfers between devices  39 us (21%)
  starting transfers between devices  27.7 us (15%)
  local copies, waits for them, and re-layouts  24.2 us (13%)
  blocking collectives  13.5 us (7%)
    dot_general x40, matrix products, matmul(): jnp.dot(left, right, precision=lax.Precision.HIGHEST, preferred_element_t...  81.4 us
    all_to_all x3, waiting for transfers between devices, tiled_gather(): lax.all_to_all(jnp.tile(shard, repeats), axis, split_axis=dim, concat_axi...  23.1 us
    slice x1, local copies, waits for them, and re-layouts, body(): jacobians[:-1]  17.5 us
    ppermute x7, waiting for transfers between devices, from_behind(): return lax.ppermute(block, axis, route)  15.9 us
    ppermute x7, starting transfers between devices, from_behind(): return lax.ppermute(block, axis, route)  14.5 us
    all_to_all x3, starting transfers between devices, tiled_gather(): lax.all_to_all(jnp.tile(shard, repeats), axis, split_axis=dim, concat_axi...  13.2 us
    all_gather x1, blocking collectives, body(): start_full = lax.all_gather(start_mine, 'col', axis=0, tiled=True)  8.01 us
    unnamed x1, blocking collectives  5.51 us
  transfers between devices with their start and end apart: 10, of which 6 were waited for; matrix products, arithmetic and copies ran while one was open for 4% of the time, Pallas kernels for 0%

profile of v1, /device:TPU:25, one launch (start us, length us, event | category | flops | bytes accessed | tf_op | source)
XLA Modules:
  0.0 188.2 jit_solution(3735531292592620661)
XLA Ops:
  0.0 17.5 %fusion.15 = (f32[11,512,512]{2,1,0:T(8,128)}, f32[11,512,512]{2,1,0:T(8,128)}) fusion(f32[12,512,512]{2,1,0:T(8,128)} %param.7), kind=kLoop, calls=%fused_computation.28 | loop fusion | bytes 46137344 | tf_op jit(solution)/shard_map/slice | solution.py:69
  17.6 49.5 %while.26 = (s32[]{:T(128)}, f32[512,128]{1,0:T(8,128)S(1)}, f32[512]{0:T(512)S(1)}, f32[11,512,512]{2,1,0:T(8,128)}, f32[11,512]{1,0:T(8,128)S(1)}, /*index=5*/s32[]{:T(128)}) while((s32[]{:T(128)}, f32[512,128]{1,0:T(8,128)S(1)}, f32[512]{0:T(512)S(1)}, f32[11,512,512]{2,1,0:T(8,128)}, f32[11,512]{1,0:T(8,128)S(1)}, ...), condition=%wide.region_1.2_spmd, body=%wide.region_0.1_spmd.sunk | while | flops 405799424 | bytes 3161161 | solution.py:39
  17.6 2.2 %fusion.50 = f32[1,512]{1,0:T(1,128)S(1)} fusion(f32[512,1]{0,1:T(1,128)S(1)} %bitcast.89, f32[11,512,512]{2,1,0:T(8,128)} %get-tuple-element.219, s32[]{:T(128)} %get-tuple-element.210), kind=kOutput, calls=%fused_computation.clone.1 | convolution fusion | flops 3145728 | bytes 1053184 | tf_op jit(solution)/shard_map/while/body/eval_jaxpr/dot_general | solution.py:22
  19.9 2.2 %fusion.49 = f32[512,128]{1,0:T(8,128)S(1)} fusion(f32[512,128]{1,0:T(8,128)S(1)} %copy.27, f32[11,512,512]{2,1,0:T(8,128)} %get-tuple-element.219, s32[]{:T(128)} %get-tuple-element.210), kind=kOutput, calls=%fused_computation.2.clone.1 | convolution fusion | flops 402653184 | bytes 1573376 | tf_op jit(solution)/shard_map/while/body/eval_jaxpr/dot_general | solution.py:22
  22.1 2.2 %fusion.50 = f32[1,512]{1,0:T(1,128)S(1)} fusion(f32[512,1]{0,1:T(1,128)S(1)} %bitcast.89, f32[11,512,512]{2,1,0:T(8,128)} %get-tuple-element.219, s32[]{:T(128)} %get-tuple-element.210), kind=kOutput, calls=%fused_computation.clone.1 | convolution fusion | flops 3145728 | bytes 1053184 | tf_op jit(solution)/shard_map/while/body/eval_jaxpr/dot_general | solution.py:22
  24.4 2.2 %fusion.49 = f32[512,128]{1,0:T(8,128)S(1)} fusion(f32[512,128]{1,0:T(8,128)S(1)} %copy.27, f32[11,512,512]{2,1,0:T(8,128)} %get-tuple-element.219, s32[]{:T(128)} %get-tuple-element.210), kind=kOutput, calls=%fused_computation.2.clone.1 | convolution fusion | flops 402653184 | bytes 1573376 | tf_op jit(solution)/shard_map/while/body/eval_jaxpr/dot_general | solution.py:22
  26.6 2.2 %fusion.50 = f32[1,512]{1,0:T(1,128)S(1)} fusion(f32[512,1]{0,1:T(1,128)S(1)} %bitcast.89, f32[11,512,512]{2,1,0:T(8,128)} %get-tuple-element.219, s32[]{:T(128)} %get-tuple-element.210), kind=kOutput, calls=%fused_computation.clone.1 | convolution fusion | flops 3145728 | bytes 1053184 | tf_op jit(solution)/shard_map/while/body/eval_jaxpr/dot_general | solution.py:22
  28.9 2.2 %fusion.49 = f32[512,128]{1,0:T(8,128)S(1)} fusion(f32[512,128]{1,0:T(8,128)S(1)} %copy.27, f32[11,512,512]{2,1,0:T(8,128)} %get-tuple-element.219, s32[]{:T(128)} %get-tuple-element.210), kind=kOutput, calls=%fused_computation.2.clone.1 | convolution fusion | flops 402653184 | bytes 1573376 | tf_op jit(solution)/shard_map/while/body/eval_jaxpr/dot_general | solution.py:22
  31.1 2.2 %fusion.50 = f32[1,512]{1,0:T(1,128)S(1)} fusion(f32[512,1]{0,1:T(1,128)S(1)} %bitcast.89, f32[11,512,512]{2,1,0:T(8,128)} %get-tuple-element.219, s32[]{:T(128)} %get-tuple-element.210), kind=kOutput, calls=%fused_computation.clone.1 | convolution fusion | flops 3145728 | bytes 1053184 | tf_op jit(solution)/shard_map/while/body/eval_jaxpr/dot_general | solution.py:22
  33.4 2.2 %fusion.49 = f32[512,128]{1,0:T(8,128)S(1)} fusion(f32[512,128]{1,0:T(8,128)S(1)} %copy.27, f32[11,512,512]{2,1,0:T(8,128)} %get-tuple-element.219, s32[]{:T(128)} %get-tuple-element.210), kind=kOutput, calls=%fused_computation.2.clone.1 | convolution fusion | flops 402653184 | bytes 1573376 | tf_op jit(solution)/shard_map/while/body/eval_jaxpr/dot_general | solution.py:22
  35.6 2.2 %fusion.50 = f32[1,512]{1,0:T(1,128)S(1)} fusion(f32[512,1]{0,1:T(1,128)S(1)} %bitcast.89, f32[11,512,512]{2,1,0:T(8,128)} %get-tuple-element.219, s32[]{:T(128)} %get-tuple-element.210), kind=kOutput, calls=%fused_computation.clone.1 | convolution fusion | flops 3145728 | bytes 1053184 | tf_op jit(solution)/shard_map/while/body/eval_jaxpr/dot_general | solution.py:22
  37.9 2.2 %fusion.49 = f32[512,128]{1,0:T(8,128)S(1)} fusion(f32[512,128]{1,0:T(8,128)S(1)} %copy.27, f32[11,512,512]{2,1,0:T(8,128)} %get-tuple-element.219, s32[]{:T(128)} %get-tuple-element.210), kind=kOutput, calls=%fused_computation.2.clone.1 | convolution fusion | flops 402653184 | bytes 1573376 | tf_op jit(solution)/shard_map/while/body/eval_jaxpr/dot_general | solution.py:22
  40.1 2.2 %fusion.50 = f32[1,512]{1,0:T(1,128)S(1)} fusion(f32[512,1]{0,1:T(1,128)S(1)} %bitcast.89, f32[11,512,512]{2,1,0:T(8,128)} %get-tuple-element.219, s32[]{:T(128)} %get-tuple-element.210), kind=kOutput, calls=%fused_computation.clone.1 | convolution fusion | flops 3145728 | bytes 1053184 | tf_op jit(solution)/shard_map/while/body/eval_jaxpr/dot_general | solution.py:22
  42.4 2.2 %fusion.49 = f32[512,128]{1,0:T(8,128)S(1)} fusion(f32[512,128]{1,0:T(8,128)S(1)} %copy.27, f32[11,512,512]{2,1,0:T(8,128)} %get-tuple-element.219, s32[]{:T(128)} %get-tuple-element.210), kind=kOutput, calls=%fused_computation.2.clone.1 | convolution fusion | flops 402653184 | bytes 1573376 | tf_op jit(solution)/shard_map/while/body/eval_jaxpr/dot_general | solution.py:22
  44.6 2.2 %fusion.50 = f32[1,512]{1,0:T(1,128)S(1)} fusion(f32[512,1]{0,1:T(1,128)S(1)} %bitcast.89, f32[11,512,512]{2,1,0:T(8,128)} %get-tuple-element.219, s32[]{:T(128)} %get-tuple-element.210), kind=kOutput, calls=%fused_computation.clone.1 | convolution fusion | flops 3145728 | bytes 1053184 | tf_op jit(solution)/shard_map/while/body/eval_jaxpr/dot_general | solution.py:22
  46.9 2.2 %fusion.49 = f32[512,128]{1,0:T(8,128)S(1)} fusion(f32[512,128]{1,0:T(8,128)S(1)} %copy.27, f32[11,512,512]{2,1,0:T(8,128)} %get-tuple-element.219, s32[]{:T(128)} %get-tuple-element.210), kind=kOutput, calls=%fused_computation.2.clone.1 | convolution fusion | flops 402653184 | bytes 1573376 | tf_op jit(solution)/shard_map/while/body/eval_jaxpr/dot_general | solution.py:22
  49.1 2.2 %fusion.50 = f32[1,512]{1,0:T(1,128)S(1)} fusion(f32[512,1]{0,1:T(1,128)S(1)} %bitcast.89, f32[11,512,512]{2,1,0:T(8,128)} %get-tuple-element.219, s32[]{:T(128)} %get-tuple-element.210), kind=kOutput, calls=%fused_computation.clone.1 | convolution fusion | flops 3145728 | bytes 1053184 | tf_op jit(solution)/shard_map/while/body/eval_jaxpr/dot_general | solution.py:22
  51.4 2.2 %fusion.49 = f32[512,128]{1,0:T(8,128)S(1)} fusion(f32[512,128]{1,0:T(8,128)S(1)} %copy.27, f32[11,512,512]{2,1,0:T(8,128)} %get-tuple-element.219, s32[]{:T(128)} %get-tuple-element.210), kind=kOutput, calls=%fused_computation.2.clone.1 | convolution fusion | flops 402653184 | bytes 1573376 | tf_op jit(solution)/shard_map/while/body/eval_jaxpr/dot_general | solution.py:22
  55.9 2.2 %fusion.49 = f32[512,128]{1,0:T(8,128)S(1)} fusion(f32[512,128]{1,0:T(8,128)S(1)} %copy.27, f32[11,512,512]{2,1,0:T(8,128)} %get-tuple-element.219, s32[]{:T(128)} %get-tuple-element.210), kind=kOutput, calls=%fused_computation.2.clone.1 | convolution fusion | flops 402653184 | bytes 1573376 | tf_op jit(solution)/shard_map/while/body/eval_jaxpr/dot_general | solution.py:22
  58.1 2.2 %fusion.50 = f32[1,512]{1,0:T(1,128)S(1)} fusion(f32[512,1]{0,1:T(1,128)S(1)} %bitcast.89, f32[11,512,512]{2,1,0:T(8,128)} %get-tuple-element.219, s32[]{:T(128)} %get-tuple-element.210), kind=kOutput, calls=%fused_computation.clone.1 | convolution fusion | flops 3145728 | bytes 1053184 | tf_op jit(solution)/shard_map/while/body/eval_jaxpr/dot_general | solution.py:22
  60.4 2.2 %fusion.49 = f32[512,128]{1,0:T(8,128)S(1)} fusion(f32[512,128]{1,0:T(8,128)S(1)} %copy.27, f32[11,512,512]{2,1,0:T(8,128)} %get-tuple-element.219, s32[]{:T(128)} %get-tuple-element.210), kind=kOutput, calls=%fused_computation.2.clone.1 | convolution fusion | flops 402653184 | bytes 1573376 | tf_op jit(solution)/shard_map/while/body/eval_jaxpr/dot_general | solution.py:22
  62.6 2.2 %fusion.50 = f32[1,512]{1,0:T(1,128)S(1)} fusion(f32[512,1]{0,1:T(1,128)S(1)} %bitcast.89, f32[11,512,512]{2,1,0:T(8,128)} %get-tuple-element.219, s32[]{:T(128)} %get-tuple-element.210), kind=kOutput, calls=%fused_computation.clone.1 | convolution fusion | flops 3145728 | bytes 1053184 | tf_op jit(solution)/shard_map/while/body/eval_jaxpr/dot_general | solution.py:22
  64.9 2.2 %fusion.49 = f32[512,128]{1,0:T(8,128)S(1)} fusion(f32[512,128]{1,0:T(8,128)S(1)} %copy.27, f32[11,512,512]{2,1,0:T(8,128)} %get-tuple-element.219, s32[]{:T(128)} %get-tuple-element.210), kind=kOutput, calls=%fused_computation.2.clone.1 | convolution fusion | flops 402653184 | bytes 1573376 | tf_op jit(solution)/shard_map/while/body/eval_jaxpr/dot_general | solution.py:22
  68.2 4.3 %all-to-all-start = ((f32[512,4,128]{2,0,1:T(8,128)}), f32[512,4,128]{2,0,1:T(8,128)S(1)}, u32[]{:S(2)}, u32[]{:S(2)}) async-start(f32[512,4,128]{2,0,1:T(8,128)} %tile.6), calls=%async_computation | async-start | bytes 2097152 | tf_op jit(solution)/shard_map/all_to_all | solution.py:10
  72.5 3.1 %collective-permute-start = (f32[512,128]{1,0:T(8,128)S(1)}, f32[512,128]{1,0:T(8,128)S(1)}, u32[]{:S(2)}, u32[]{:S(2)}) collective-permute-start(f32[512,128]{1,0:T(8,128)S(1)} %get-tuple-element.107), channel_id=1, source_target_pairs={{0,4},{4,8},{8,12},{12,16},{16,20},{20,24},{24,28},{1,5},{5,9},{9,... | collective-permute-start | bytes 786440 | tf_op jit(solution)/shard_map/ppermute | solution.py:18
  75.6 10.3 %all-to-all-done = f32[512,4,128]{2,0,1:T(8,128)S(1)} async-done(((f32[512,4,128]{2,0,1:T(8,128)}), f32[512,4,128]{2,0,1:T(8,128)S(1)}, u32[]{:S(2)}, u32[]{:S(2)}) %all-to-all-start) | async-done | bytes 1048608 | tf_op jit(solution)/shard_map/all_to_all | solution.py:10
  89.2 4.5 %all-to-all-start.1 = ((f32[512,4,128]{2,0,1:T(8,128)}), f32[512,4,128]{2,0,1:T(8,128)S(1)}, u32[]{:S(2)}, u32[]{:S(2)}) async-start(f32[512,4,128]{2,0,1:T(8,128)} %tile.7), calls=%async_computation.1 | async-start | bytes 2097152 | tf_op jit(solution)/shard_map/all_to_all | solution.py:10
  95.0 3.1 %collective-permute-start.3 = (f32[512]{0:T(512)S(1)}, f32[512]{0:T(512)S(1)}, u32[]{:S(2)}, u32[]{:S(2)}) collective-permute-start(f32[512]{0:T(512)S(1)} %get-tuple-element.108), channel_id=1, source_target_pairs={{0,4},{4,8},{8,12},{12,16},{16,20},{20,24},{24,28},{1,5},{5,9},{9,... | collective-permute-start | bytes 6152 | tf_op jit(solution)/shard_map/ppermute | solution.py:18
  98.1 9.0 %all-to-all-done.1 = f32[512,4,128]{2,0,1:T(8,128)S(1)} async-done(((f32[512,4,128]{2,0,1:T(8,128)}), f32[512,4,128]{2,0,1:T(8,128)S(1)}, u32[]{:S(2)}, u32[]{:S(2)}) %all-to-all-start.1) | async-done | bytes 1048608 | tf_op jit(solution)/shard_map/all_to_all | solution.py:10
  107.5 2.8 %convolution_select_fusion.1 = f32[512,128]{1,0:T(8,128)S(1)} fusion(f32[512,128]{1,0:T(8,128)} %copy-done, f32[512,512]{0,1:T(8,128)S(1)} %bitcast.81, f32[512,128]{1,0:T(8,128)} %collective-permute-done.1, pred[]{:T(512)S(6)} %ge.10), kind=kOutput, calls=%fused_computation.16 | convolution fusion | flops 402718720 | bytes 1835009 | tf_op jit(solution)/shard_map/dot_general | solution.py:22
  111.4 4.5 %all-to-all-start.2 = ((f32[512,4,128]{2,0,1:T(8,128)}), f32[512,4,128]{2,0,1:T(8,128)S(1)}, u32[]{:S(2)}, u32[]{:S(2)}) async-start(f32[512,4,128]{2,0,1:T(8,128)} %tile.8), calls=%async_computation.2 | async-start | bytes 2097152 | tf_op jit(solution)/shard_map/all_to_all | solution.py:10
  117.8 3.3 %collective-permute-done.4 = f32[512]{0:T(512)S(1)} collective-permute-done((f32[512]{0:T(512)S(1)}, f32[512]{0:T(512)S(1)}, u32[]{:S(2)}, u32[]{:S(2)}) %collective-permute-start.4) | collective-permute-done | bytes 2080 | tf_op jit(solution)/shard_map/ppermute | solution.py:18
  125.6 3.7 %all-to-all-done.2 = f32[512,4,128]{2,0,1:T(8,128)S(1)} async-done(((f32[512,4,128]{2,0,1:T(8,128)}), f32[512,4,128]{2,0,1:T(8,128)S(1)}, u32[]{:S(2)}, u32[]{:S(2)}) %all-to-all-start.2) | async-done | bytes 1048608 | tf_op jit(solution)/shard_map/all_to_all | solution.py:10
  130.3 10.5 %collective-permute-done.2 = f32[512,128]{1,0:T(8,128)S(1)} collective-permute-done((f32[512,128]{1,0:T(8,128)S(1)}, f32[512,128]{1,0:T(8,128)S(1)}, u32[]{:S(2)}, u32[]{:S(2)}) %collective-permute-start.2) | collective-permute-done | bytes 262176 | tf_op jit(solution)/shard_map/ppermute | solution.py:18
  143.0 5.5 %all-reduce = f32[512]{0:T(512)S(1)} all-reduce(f32[512]{0:T(512)S(1)} %bitcast.96), channel_id=2, replica_groups=mesh['tm'=8,'col'=4] {'col'}, use_global_device_ids=true, to_apply=%region_2.3.clone | all-reduce | flops 512 | bytes 4096
  148.6 3.1 %collective-permute-start.6 = (f32[128]{0:T(128)S(1)}, f32[128]{0:T(128)S(1)}, u32[]{:S(2)}, u32[]{:S(2)}) collective-permute-start(f32[128]{0:T(128)S(1)} %dynamic-slice_add_fusion), channel_id=1, source_target_pairs={{0,4},{4,8},{8,12},{12,16},{16,20},{20,24},{24,28},{1,5},{5,9},{9,... | collective-permute-start | bytes 1544 | tf_op jit(solution)/shard_map/ppermute | solution.py:18
  153.8 8.0 %all-gather = f32[4,1,128]{2,1,0:T(1,128)S(1)} all-gather(f32[1,1,128]{2,1,0:T(1,128)S(1)} %fusion.12), channel_id=1, replica_groups=mesh['tm'=8,'col'=4] {'col'}, dimensions={0}, use_global_device_ids=true | all-gather | bytes 2560 | tf_op jit(solution)/shard_map/all_gather | solution.py:62
  161.8 25.8 %while.27 = (s32[]{:T(128)}, f32[512]{0:T(512)S(1)}, f32[11,128]{1,0:T(8,128)S(1)}, f32[11,512,512]{2,1,0:T(8,128)}, f32[11,512]{1,0:T(8,128)S(1)}, /*index=5*/s32[]{:T(128)}, s32[]{:T(128)}, s32[]{:T(128)}) while((s32[]{:T(128)}, f32[512]{0:T(512)S(1)}, f32[11,128]{1,0:T(8,128)S(1)}, f32[11,512,512]{2,1,0:T(8,128)}, f32[11,512]{1,0:T(8,128)S(1)}, ...), condition=%wide.region_4.5_spmd, body=%wide.region_3.4_spmd.sunk | while | flops 3146242 | bytes 1065569 | solution.py:69
  164.1 2.2 %fusion.53 = f32[1,512]{1,0:T(1,128)S(1)} fusion(f32[512,1]{0,1:T(1,128)S(1)} %bitcast.92, f32[11,512,512]{2,1,0:T(8,128)} %get-tuple-element.241, s32[]{:T(128)} %get-tuple-element.230), kind=kOutput, calls=%fused_computation.9.clone.1 | convolution fusion | flops 3145728 | bytes 1053184 | tf_op jit(solution)/shard_map/while/body/eval_jaxpr/dot_general | solution.py:22
  166.5 2.2 %fusion.53 = f32[1,512]{1,0:T(1,128)S(1)} fusion(f32[512,1]{0,1:T(1,128)S(1)} %bitcast.92, f32[11,512,512]{2,1,0:T(8,128)} %get-tuple-element.241, s32[]{:T(128)} %get-tuple-element.230), kind=kOutput, calls=%fused_computation.9.clone.1 | convolution fusion | flops 3145728 | bytes 1053184 | tf_op jit(solution)/shard_map/while/body/eval_jaxpr/dot_general | solution.py:22
  168.8 2.2 %fusion.53 = f32[1,512]{1,0:T(1,128)S(1)} fusion(f32[512,1]{0,1:T(1,128)S(1)} %bitcast.92, f32[11,512,512]{2,1,0:T(8,128)} %get-tuple-element.241, s32[]{:T(128)} %get-tuple-element.230), kind=kOutput, calls=%fused_computation.9.clone.1 | convolution fusion | flops 3145728 | bytes 1053184 | tf_op jit(solution)/shard_map/while/body/eval_jaxpr/dot_general | solution.py:22
  171.2 2.2 %fusion.53 = f32[1,512]{1,0:T(1,128)S(1)} fusion(f32[512,1]{0,1:T(1,128)S(1)} %bitcast.92, f32[11,512,512]{2,1,0:T(8,128)} %get-tuple-element.241, s32[]{:T(128)} %get-tuple-element.230), kind=kOutput, calls=%fused_computation.9.clone.1 | convolution fusion | flops 3145728 | bytes 1053184 | tf_op jit(solution)/shard_map/while/body/eval_jaxpr/dot_general | solution.py:22
  173.5 2.2 %fusion.53 = f32[1,512]{1,0:T(1,128)S(1)} fusion(f32[512,1]{0,1:T(1,128)S(1)} %bitcast.92, f32[11,512,512]{2,1,0:T(8,128)} %get-tuple-element.241, s32[]{:T(128)} %get-tuple-element.230), kind=kOutput, calls=%fused_computation.9.clone.1 | convolution fusion | flops 3145728 | bytes 1053184 | tf_op jit(solution)/shard_map/while/body/eval_jaxpr/dot_general | solution.py:22
  175.9 2.2 %fusion.53 = f32[1,512]{1,0:T(1,128)S(1)} fusion(f32[512,1]{0,1:T(1,128)S(1)} %bitcast.92, f32[11,512,512]{2,1,0:T(8,128)} %get-tuple-element.241, s32[]{:T(128)} %get-tuple-element.230), kind=kOutput, calls=%fused_computation.9.clone.1 | convolution fusion | flops 3145728 | bytes 1053184 | tf_op jit(solution)/shard_map/while/body/eval_jaxpr/dot_general | solution.py:22
  178.2 2.2 %fusion.53 = f32[1,512]{1,0:T(1,128)S(1)} fusion(f32[512,1]{0,1:T(1,128)S(1)} %bitcast.92, f32[11,512,512]{2,1,0:T(8,128)} %get-tuple-element.241, s32[]{:T(128)} %get-tuple-element.230), kind=kOutput, calls=%fused_computation.9.clone.1 | convolution fusion | flops 3145728 | bytes 1053184 | tf_op jit(solution)/shard_map/while/body/eval_jaxpr/dot_general | solution.py:22
  180.6 2.2 %fusion.53 = f32[1,512]{1,0:T(1,128)S(1)} fusion(f32[512,1]{0,1:T(1,128)S(1)} %bitcast.92, f32[11,512,512]{2,1,0:T(8,128)} %get-tuple-element.241, s32[]{:T(128)} %get-tuple-element.230), kind=kOutput, calls=%fused_computation.9.clone.1 | convolution fusion | flops 3145728 | bytes 1053184 | tf_op jit(solution)/shard_map/while/body/eval_jaxpr/dot_general | solution.py:22
  182.9 2.2 %fusion.53 = f32[1,512]{1,0:T(1,128)S(1)} fusion(f32[512,1]{0,1:T(1,128)S(1)} %bitcast.92, f32[11,512,512]{2,1,0:T(8,128)} %get-tuple-element.241, s32[]{:T(128)} %get-tuple-element.230), kind=kOutput, calls=%fused_computation.9.clone.1 | convolution fusion | flops 3145728 | bytes 1053184 | tf_op jit(solution)/shard_map/while/body/eval_jaxpr/dot_general | solution.py:22
  185.3 2.2 %fusion.53 = f32[1,512]{1,0:T(1,128)S(1)} fusion(f32[512,1]{0,1:T(1,128)S(1)} %bitcast.92, f32[11,512,512]{2,1,0:T(8,128)} %get-tuple-element.241, s32[]{:T(128)} %get-tuple-element.230), kind=kOutput, calls=%fused_computation.9.clone.1 | convolution fusion | flops 3145728 | bytes 1053184 | tf_op jit(solution)/shard_map/while/body/eval_jaxpr/dot_general | solution.py:22
  (122 shorter events, 25.0 us)
Async XLA Ops:
  0.0 17.5 %copy-start.1 = (f32[12,512]{1,0:T(8,128)S(1)}, f32[12,512]{1,0:T(8,128)}, u32[]{:S(2)}) copy-start(f32[12,512]{1,0:T(8,128)} %param.8) | copy-start | bytes 73732
  0.0 17.6 %slice-start = ((f32[12,512,512]{2,1,0:T(8,128)}), f32[1,512,512]{2,1,0:T(8,128)S(1)}, s32[]{:S(2)}) async-start(f32[12,512,512]{2,1,0:T(8,128)} %param.7), calls=%async_computation.3 | async-start | bytes 2097152 | tf_op jit(solution)/shard_map/slice | solution.py:40
  0.0 17.6 %slice-start.1 = ((f32[12,512]{1,0:T(8,128)}), f32[1,512]{1,0:T(1,128)S(1)}, s32[]{:S(2)}) async-start(f32[12,512]{1,0:T(8,128)} %param.8), calls=%async_computation.4 | async-start | bytes 4096 | tf_op jit(solution)/shard_map/slice | solution.py:40
  67.1 55.9 %copy-start.3 = (u32[32]{0:T(128)S(1)}, u32[32]{0:T(128)}, u32[]{:S(2)}) copy-start(u32[32]{0:T(128)} %constant.58) | copy-start | bytes 388
  68.2 74.4 %copy-start.2 = (f32[128]{0:T(128)S(1)}, f32[128]{0:T(128)}, u32[]{:S(2)}) copy-start(f32[128]{0:T(128)} %param.9) | copy-start | bytes 1540
  68.2 17.8 %all-to-all-start = ((f32[512,4,128]{2,0,1:T(8,128)}), f32[512,4,128]{2,0,1:T(8,128)S(1)}, u32[]{:S(2)}, u32[]{:S(2)}) async-start(f32[512,4,128]{2,0,1:T(8,128)} %tile.6), calls=%async_computation | async-start | bytes 2097152 | tf_op jit(solution)/shard_map/all_to_all | solution.py:10
  72.5 13.8 %collective-permute-start = (f32[512,128]{1,0:T(8,128)S(1)}, f32[512,128]{1,0:T(8,128)S(1)}, u32[]{:S(2)}, u32[]{:S(2)}) collective-permute-start(f32[512,128]{1,0:T(8,128)S(1)} %get-tuple-element.107), channel_id=1, source_target_pairs={{0,4},{4,8},{8,12},{12,16},{16,20},{20,24},{24,28},{1,5},{5,9},{9,... | collective-permute-start | bytes 786440 | tf_op jit(solution)/shard_map/ppermute | solution.py:18
  88.1 19.4 %copy-start = (f32[512,128]{1,0:T(8,128)}, f32[512,128]{1,0:T(8,128)S(1)}, u32[]{:S(2)}) copy-start(f32[512,128]{1,0:T(8,128)S(1)} %convolution_select_fusion.2) | copy-start | bytes 786436
  89.2 17.9 %all-to-all-start.1 = ((f32[512,4,128]{2,0,1:T(8,128)}), f32[512,4,128]{2,0,1:T(8,128)S(1)}, u32[]{:S(2)}, u32[]{:S(2)}) async-start(f32[512,4,128]{2,0,1:T(8,128)} %tile.7), calls=%async_computation.1 | async-start | bytes 2097152 | tf_op jit(solution)/shard_map/all_to_all | solution.py:10
  93.7 13.8 %collective-permute-start.1 = (f32[512,128]{1,0:T(8,128)S(1)}, f32[512,128]{1,0:T(8,128)}, u32[]{:S(2)}, u32[]{:S(2)}) collective-permute-start(f32[512,128]{1,0:T(8,128)S(1)} %convolution_select_fusion.2), channel_id=1, source_target_pairs={{0,8},{4,12},{8,16},{12,20},{16,24},{20,28},{1,9},{5,13},{9,17},{1... | collective-permute-start | bytes 786440 | tf_op jit(solution)/shard_map/ppermute | solution.py:18
  95.0 20.8 %collective-permute-start.3 = (f32[512]{0:T(512)S(1)}, f32[512]{0:T(512)S(1)}, u32[]{:S(2)}, u32[]{:S(2)}) collective-permute-start(f32[512]{0:T(512)S(1)} %get-tuple-element.108), channel_id=1, source_target_pairs={{0,4},{4,8},{8,12},{12,16},{16,20},{20,24},{24,28},{1,5},{5,9},{9,... | collective-permute-start | bytes 6152 | tf_op jit(solution)/shard_map/ppermute | solution.py:18
  111.4 17.9 %all-to-all-start.2 = ((f32[512,4,128]{2,0,1:T(8,128)}), f32[512,4,128]{2,0,1:T(8,128)S(1)}, u32[]{:S(2)}, u32[]{:S(2)}) async-start(f32[512,4,128]{2,0,1:T(8,128)} %tile.8), calls=%async_computation.2 | async-start | bytes 2097152 | tf_op jit(solution)/shard_map/all_to_all | solution.py:10
  116.5 4.6 %collective-permute-start.4 = (f32[512]{0:T(512)S(1)}, f32[512]{0:T(512)S(1)}, u32[]{:S(2)}, u32[]{:S(2)}) collective-permute-start(f32[512]{0:T(512)S(1)} %add_select_fusion.2), channel_id=1, source_target_pairs={{0,8},{4,12},{8,16},{12,20},{16,24},{20,28},{1,9},{5,13},{9,17},{1... | collective-permute-start | bytes 6152 | tf_op jit(solution)/shard_map/ppermute | solution.py:18
  121.7 7.9 %collective-permute-start.5 = (f32[512]{0:T(512)S(1)}, f32[512]{0:T(512)S(1)}, u32[]{:S(2)}, u32[]{:S(2)}) collective-permute-start(f32[512]{0:T(512)S(1)} %add_select_fusion.1), channel_id=1, source_target_pairs={{0,16},{4,20},{8,24},{12,28},{1,17},{5,21},{9,25},{13,29},{2,18},{... | collective-permute-start | bytes 6152 | tf_op jit(solution)/shard_map/ppermute | solution.py:18
  124.3 16.5 %collective-permute-start.2 = (f32[512,128]{1,0:T(8,128)S(1)}, f32[512,128]{1,0:T(8,128)S(1)}, u32[]{:S(2)}, u32[]{:S(2)}) collective-permute-start(f32[512,128]{1,0:T(8,128)S(1)} %convolution_select_fusion.1), channel_id=1, source_target_pairs={{0,16},{4,20},{8,24},{12,28},{1,17},{5,21},{9,25},{13,29},{2,18},{... | collective-permute-start | bytes 786440 | tf_op jit(solution)/shard_map/ppermute | solution.py:18
  148.6 5.2 %collective-permute-start.6 = (f32[128]{0:T(128)S(1)}, f32[128]{0:T(128)S(1)}, u32[]{:S(2)}, u32[]{:S(2)}) collective-permute-start(f32[128]{0:T(128)S(1)} %dynamic-slice_add_fusion), channel_id=1, source_target_pairs={{0,4},{4,8},{8,12},{12,16},{16,20},{20,24},{24,28},{1,5},{5,9},{9,... | collective-permute-start | bytes 1544 | tf_op jit(solution)/shard_map/ppermute | solution.py:18
